TPU v7x, 32 devices: a whole 2x2x4 slice. The times are simulated.
32 devices in a mesh: row: 4 (over z), col: 8 (over y, x, core).
Axes of the slice: x: 2, y: 2, z: 4, core: 2. Of those that a mesh axis runs over, the one named last changes fastest.
Arguments:
- block_cells: float32 [352, 5, 16, 256], P(('row', 'col')), may hold values from -0.6 to 1.4, as said below
- slot_blocks: int32 [32, 11], replicated, may hold values from -1 to 191, as said below
Outputs:
- new_cells: float32 [224, 5, 16, 256], P(('row', 'col'))
Inputs may be any that keep to these rules, and one draw needn't show every extreme that they name: `slot_blocks`: row r * 8 + c lists the blocks held by device (r, c): block ids first, in slot order, then -1. Block b belongs to column group b // 24, and every block of column group c is held by exactly one device of that column group. Each device holds 1 to 11 blocks, the devices of a column group hold 24 blocks together, and in every column group one device holds 11 blocks and one holds 1. `block_cells`: fields 0 and 4 (density, pressure) lie in 0.7 to 1.4 and fields 1 to 3 (velocity) in -0.6 to 0.6. Slots marked -1 in slot_blocks hold values that no output depends on.
All inputs are finite; a program needn't handle non-finite values.
Results may differ from a plain program's by a relative error of at most 0.0001.
Values sent between devices are 32-bit elements; how exact they have to be, the bound alone decides.
A program may use at most 64 MiB of HBM per device.

v0:
```python
import jax
import jax.numpy as jnp
from jax import lax
from jax.sharding import PartitionSpec as P

BLK_MEAN = 6
OUT = 7
heat_ratio = 1.4
time_step = 0.12
thermal_leading_multiplier = 0.2
thermal_power_law_index = 0.7


def swapped(array, axis, apart):
    return lax.ppermute(array, axis, [(i, i ^ 1 << apart) for i in range(lax.axis_size(axis))])


def from_behind(block, axis, distance):
    devices = range(lax.axis_size(axis))
    route = [((i - distance) % len(devices), i) for i in devices]
    return lax.ppermute(block, axis, route)


def rebalance_table(anchors, counts):
    row_count, columns, slot_width = anchors.shape
    slot_ids = jnp.arange(slot_width, dtype=jnp.int32)
    row_ids = jnp.arange(row_count, dtype=jnp.int32)
    for section_bit in range(row_count.bit_length() - 1):
        partner = row_ids ^ 1 << section_bit
        other_anchors = anchors[partner]
        other_counts = counts[partner]
        sending = jnp.maximum(counts - other_counts, 0) // 2
        taking = jnp.maximum(other_counts - counts, 0) // 2
        keeping = (counts - sending)[:, :, None]
        anchor_slot = other_counts[:, :, None] - taking[:, :, None] + slot_ids - keeping
        pulled = jnp.take_along_axis(
            other_anchors, jnp.clip(anchor_slot, 0, slot_width - 1), axis=2
        )
        anchors = jnp.where(
            slot_ids < keeping,
            anchors,
            jnp.where(slot_ids < keeping + taking[:, :, None], pulled, -1),
        )
        counts = counts - sending + taking
    return (anchors, counts)


def to_conserved(primitive):
    matter_per_volume = primitive[0]
    velocity = primitive[1:4]
    fluid_static_stress = primitive[4]
    energy = fluid_static_stress / (heat_ratio - 1.0) + 0.5 * matter_per_volume * jnp.sum(
        velocity * velocity, axis=0
    )
    return jnp.concatenate(
        [matter_per_volume[None], matter_per_volume[None] * velocity, energy[None]], axis=0
    )


def to_primitive(conserved):
    matter_per_volume = conserved[0]
    velocity = conserved[1:4] / matter_per_volume
    fluid_static_stress = (heat_ratio - 1.0) * (
        conserved[4] - 0.5 * matter_per_volume * jnp.sum(velocity * velocity, axis=0)
    )
    return jnp.concatenate([matter_per_volume[None], velocity, fluid_static_stress[None]], axis=0)


def cell_terms(conserved, normal):
    matter_per_volume = conserved[0]
    momentum = conserved[1:4]
    velocity = momentum / matter_per_volume
    fluid_static_stress = (heat_ratio - 1.0) * (
        conserved[4] - 0.5 * matter_per_volume * jnp.sum(velocity * velocity, axis=0)
    )
    perpendicular_flow_rate = velocity[normal]
    moment_flux = momentum * perpendicular_flow_rate
    moment_flux = moment_flux.at[normal].add(fluid_static_stress)
    face_transport_amounts = jnp.concatenate(
        [
            momentum[normal][None],
            moment_flux,
            ((conserved[4] + fluid_static_stress) * perpendicular_flow_rate)[None],
        ],
        axis=0,
    )
    sound_signal_rate = jnp.sqrt(heat_ratio * fluid_static_stress / matter_per_volume)
    fluid_thermal_state = fluid_static_stress / matter_per_volume
    thermal_diffusivity_factor = thermal_leading_multiplier * jnp.power(
        fluid_thermal_state, thermal_power_law_index
    )
    return (
        face_transport_amounts,
        jnp.abs(perpendicular_flow_rate) + sound_signal_rate,
        fluid_thermal_state,
        thermal_diffusivity_factor,
        fluid_static_stress,
    )


def face_flux(lower_cons, lower_data, upper_cons, upper_data):
    wave_speed = jnp.maximum(lower_data[1], upper_data[1])
    face_transport_amounts = 0.5 * (lower_data[0] + upper_data[0]) - 0.5 * wave_speed[None] * (
        upper_cons - lower_cons
    )
    heat_flow = 0.5 * (lower_data[3] + upper_data[3]) * (upper_data[2] - lower_data[2])
    return face_transport_amounts.at[4].add(-heat_flow)


def wall_flux(fluid_static_stress, normal):
    nothing = jnp.zeros_like(fluid_static_stress)
    members = [nothing, nothing, nothing, nothing, nothing]
    members[normal + 1] = fluid_static_stress
    return jnp.stack(members, axis=0)


def cut_rows(tree, first_index, last_index):
    return jax.tree.map(lambda member: member[..., first_index:last_index, :], tree)


def cut_flat(tree, first_index, last_index):
    return jax.tree.map(lambda member: member[..., first_index:last_index], tree)


def block_tendency(conserved, low_x, high_x, low_y, high_y):
    block_edge = conserved.shape[1]
    flat_size = conserved.shape[2]
    padded_x = jnp.concatenate([low_x, conserved, high_x], axis=1)
    cell_data = cell_terms(padded_x, 0)
    face_transport_amounts = face_flux(
        padded_x[:, :-1],
        cut_rows(cell_data, 0, block_edge + 1),
        padded_x[:, 1:],
        cut_rows(cell_data, 1, block_edge + 2),
    )
    change_x = face_transport_amounts[:, 1:] - face_transport_amounts[:, :-1]
    padded_y = jnp.concatenate([low_y, conserved, high_y], axis=2)
    cell_data = cell_terms(padded_y, 1)
    reach_end = flat_size + block_edge
    face_transport_amounts = face_flux(
        padded_y[..., :reach_end],
        cut_flat(cell_data, 0, reach_end),
        padded_y[..., block_edge:],
        cut_flat(cell_data, block_edge, reach_end + block_edge),
    )
    change_y = face_transport_amounts[..., block_edge:] - face_transport_amounts[..., :flat_size]
    cell_data = cell_terms(conserved, 2)
    interior = face_flux(
        conserved[..., :-1],
        cut_flat(cell_data, 0, flat_size - 1),
        conserved[..., 1:],
        cut_flat(cell_data, 1, flat_size),
    )
    nothing = jnp.zeros_like(interior[..., :1])
    wall_values = wall_flux(cell_data[4], 2)
    height = jnp.arange(flat_size, dtype=jnp.int32) % block_edge
    upper_face = jnp.where(
        height == block_edge - 1, wall_values, jnp.concatenate([interior, nothing], axis=-1)
    )
    lower_face = jnp.where(height == 0, wall_values, jnp.concatenate([nothing, interior], axis=-1))
    change_z = upper_face - lower_face
    return -(change_x + change_y + change_z)


def body(block_cells, slot_blocks):
    row_count = lax.axis_size("row")
    columns = lax.axis_size("col")
    my_row = lax.axis_index("row")
    my_col = lax.axis_index("col")
    slot_width = slot_blocks.shape[1]
    per_group = BLK_MEAN * row_count
    send_slots = BLK_MEAN - 1
    block_edge = block_cells.shape[2]
    flat_size = block_cells.shape[3]
    every_slot = slot_blocks.reshape(-1)
    occupied = slot_blocks >= 0
    counts = jnp.sum(occupied.astype(jnp.int32), axis=1).reshape(row_count, columns)
    device_ids = jnp.arange(row_count * columns, dtype=jnp.int32)[:, None]
    anchors = jnp.where(
        occupied, device_ids * slot_width + jnp.arange(slot_width, dtype=jnp.int32)[None, :], -1
    )
    anchors = anchors.reshape(row_count, columns, slot_width)
    final_anchors, final_counts = rebalance_table(anchors, counts)
    final_anchors = final_anchors[:, :, :OUT]
    my_anchors = final_anchors[my_row, my_col]
    row_ids = jnp.arange(row_count, dtype=jnp.int32)
    holding = block_cells
    counts_now = counts
    slot_ids = jnp.arange(slot_width, dtype=jnp.int32)
    for section_bit in range(row_count.bit_length() - 1):
        partner = row_ids ^ 1 << section_bit
        other_counts = counts_now[partner]
        sending = jnp.maximum(counts_now - other_counts, 0) // 2
        taking = jnp.maximum(other_counts - counts_now, 0) // 2
        keeping = counts_now[my_row, my_col] - sending[my_row, my_col]
        send_from = jnp.clip(keeping + jnp.arange(send_slots, dtype=jnp.int32), 0, slot_width - 1)
        outgoing = jnp.take(holding, send_from, axis=0)
        incoming = swapped(outgoing, "row", section_bit)
        candidates = jnp.concatenate([holding, incoming], axis=0)
        chosen = jnp.where(
            slot_ids < keeping,
            slot_ids,
            slot_width + jnp.clip(slot_ids - keeping, 0, send_slots - 1),
        )
        holding = jnp.take(candidates, chosen, axis=0)
        counts_now = counts_now - sending + taking
    holding = holding[:OUT]
    active = my_anchors >= 0
    benign = jnp.array([1.0, 0.0, 0.0, 0.0, 1.0], jnp.float32)[None, :, None, None]
    holding = jnp.where(active[:, None, None, None], holding, benign)
    initial = jax.vmap(to_conserved)(holding)
    my_blocks = every_slot[jnp.maximum(my_anchors, 0)]
    along_y = jnp.clip(my_blocks - my_col * per_group, 0, per_group - 1)
    below_col = (my_col - 1) % columns
    above_col = (my_col + 1) % columns

    def located(column, wanted):
        anchors_here = final_anchors[:, column].reshape(-1)
        blocks_here = jnp.where(anchors_here >= 0, every_slot[jnp.maximum(anchors_here, 0)], -1)
        return jnp.argmax(blocks_here[None, :] == wanted[:, None], axis=1)

    from_x_low = located(below_col, below_col * per_group + along_y)
    from_y_low = located(below_col, below_col * per_group + (along_y - 1) % per_group)
    from_x_high = located(above_col, above_col * per_group + along_y)
    from_y_high = located(above_col, above_col * per_group + (along_y + 1) % per_group)

    def section_rate(current):
        highs = jnp.stack(
            [
                current[:, :, block_edge - 1, :],
                current[:, :, :, flat_size - block_edge :].reshape(OUT, 5, flat_size),
            ],
            axis=1,
        )
        lows = jnp.stack(
            [current[:, :, 0, :], current[:, :, :, :block_edge].reshape(OUT, 5, flat_size)], axis=1
        )
        passed_highs = from_behind(highs, "col", 1)
        passed_lows = from_behind(lows, "col", -1)
        from_below, from_above = (
            lax.all_gather(passed_highs, "row", axis=0, tiled=True),
            lax.all_gather(passed_lows, "row", axis=0, tiled=True),
        )
        low_x = from_below[from_x_low, 0][:, :, None, :]
        low_y = from_below[from_y_low, 1].reshape(OUT, 5, block_edge, block_edge)
        high_x = from_above[from_x_high, 0][:, :, None, :]
        high_y = from_above[from_y_high, 1].reshape(OUT, 5, block_edge, block_edge)
        return jax.vmap(block_tendency)(current, low_x, high_x, low_y, high_y)

    first_section = initial + time_step * section_rate(initial)
    second_section = 0.75 * initial + 0.25 * (
        first_section + time_step * section_rate(first_section)
    )
    third_section = 1.0 / 3.0 * initial + 2.0 / 3.0 * (
        second_section + time_step * section_rate(second_section)
    )
    result = jax.vmap(to_primitive)(third_section)
    return jnp.where(active[:, None, None, None], result, jnp.zeros_like(result)).astype(
        jnp.float32
    )


def solution(mesh):
    in_specs = (P(("row", "col"), None, None, None), P())
    out_specs = P(("row", "col"), None, None, None)
    return jax.shard_map(body, mesh=mesh, in_specs=in_specs, out_specs=out_specs, check_vma=False)
```

profile of v0, /device:TPU:0, one launch (start us, length us, event | category | flops | bytes accessed | tf_op | source)
XLA Modules:
  0.0 179.7 jit_solution(13251556273873494992)
XLA Ops:
  0.0 0.8 copy.142
  7.2 1.7 gather_fusion.21
  9.0 3.1 %collective-permute-start = (f32[5,5,16,256]{3,2,1,0:T(8,128)S(1)}, f32[5,5,16,256]{3,2,1,0:T(8,128)S(1)}, u32[]{:S(2)}, u32[]{:S(2)}) collective-permute-start(f32[5,5,16,256]{3,2,1,0:T(8,128)S(1)} %broadcast_select_fusion.2), channel_id=1, source_target_pairs={{0,8},{8,0},{16,24},{24,16},{1,9},{9,1},{17,25},{25,17},{2,10},{10... | collective-permute-start | bytes 1228808 | tf_op jit(solution)/shard_map/ppermute | solution.py:15
  13.4 4.0 %gather_fusion.19 = s32[352]{0:T(512)S(1)} fusion(s32[4,8,11]{2,1,0:T(8,128)S(1)} %gather_fusion.2, s32[352]{0:T(512)S(1)} %reshape.1164), kind=kCustom, calls=%fused_computation.clone | custom fusion | bytes 7040 | tf_op jit(solution)/shard_map/jit(take_along_axis)/gather | solution.py:36
  18.2 4.0 %gather_fusion.20 = s32[352]{0:T(512)S(1)} fusion(s32[4,8,11]{2,1,0:T(8,128)S(1)} %gather_fusion.3, s32[352]{0:T(512)S(1)} %reshape.1169), kind=kCustom, calls=%fused_computation.3.clone | custom fusion | bytes 7040 | tf_op jit(solution)/shard_map/jit(take_along_axis)/gather | solution.py:36
  22.9 0.7 gather_fusion.7
  23.6 0.7 gather_fusion.4
  25.0 0.7 iota_reduce_fusion.2
  26.5 0.7 iota_reduce_fusion.3
  29.5 2.7 %collective-permute-start.1 = (f32[5,5,16,256]{3,2,1,0:T(8,128)S(1)}, f32[5,5,16,256]{3,2,1,0:T(8,128)S(1)}, u32[]{:S(2)}, u32[]{:S(2)}) collective-permute-start(f32[5,5,16,256]{3,2,1,0:T(8,128)S(1)} %broadcast_select_fusion.1), channel_id=1, source_target_pairs={{0,16},{8,24},{16,0},{24,8},{1,17},{9,25},{17,1},{25,9},{2,18},{10... | collective-permute-start | bytes 1228808 | tf_op jit(solution)/shard_map/ppermute | solution.py:15
  32.1 17.8 %collective-permute-done.1 = f32[5,5,16,256]{3,2,1,0:T(8,128)S(1)} collective-permute-done((f32[5,5,16,256]{3,2,1,0:T(8,128)S(1)}, f32[5,5,16,256]{3,2,1,0:T(8,128)S(1)}, u32[]{:S(2)}, u32[]{:S(2)}) %collective-permute-start.1) | collective-permute-done | bytes 409632 | tf_op jit(solution)/shard_map/ppermute | solution.py:15
  52.2 2.2 %collective-permute-start.3 = (f32[7,2,5,256]{3,1,2,0:T(2,128)S(1)}, f32[7,2,5,256]{3,1,2,0:T(2,128)S(1)}, u32[]{:S(2)}, u32[]{:S(2)}) collective-permute-start(f32[7,2,5,256]{3,1,2,0:T(2,128)S(1)} %pad_maximum_fusion.29), channel_id=1, source_target_pairs={{1,0},{2,1},{3,2},{4,3},{5,4},{6,5},{7,6},{0,7},{9,8},{10,9},{11,1... | collective-permute-start | bytes 215048 | tf_op jit(solution)/shard_map/ppermute | solution.py:21
  55.1 4.1 %collective-permute-done.2 = f32[7,2,5,256]{3,1,2,0:T(2,128)S(1)} collective-permute-done((f32[7,2,5,256]{3,1,2,0:T(2,128)S(1)}, f32[7,2,5,256]{3,1,2,0:T(2,128)S(1)}, u32[]{:S(2)}, u32[]{:S(2)}) %collective-permute-start.2) | collective-permute-done | bytes 71712 | tf_op jit(solution)/shard_map/ppermute | solution.py:21
  59.2 14.6 %all_gather.18 = f32[28,2,5,256]{3,1,2,0:T(2,128)S(1)} all-gather(f32[7,2,5,256]{3,1,2,0:T(2,128)S(1)} %collective-permute-done.2), channel_id=1, replica_groups=mesh['row'=4,'col'=8] {'row'}, dimensions={0}, use_global_device_ids=true | all-gather | bytes 358400 | tf_op jit(solution)/shard_map/all_gather | solution.py:241
  74.4 13.9 %all_gather.19 = f32[28,2,5,256]{3,1,2,0:T(2,128)S(1)} all-gather(f32[7,2,5,256]{3,1,2,0:T(2,128)S(1)} %collective-permute-done.3), channel_id=1, replica_groups=mesh['row'=4,'col'=8] {'row'}, dimensions={0}, use_global_device_ids=true | all-gather | bytes 358400 | tf_op jit(solution)/shard_map/all_gather | solution.py:242
  90.4 1.6 gather_fusion.8
  96.8 0.7 collective-permute-start.4
  98.1 3.6 %collective-permute-done.4 = f32[7,2,5,256]{3,1,2,0:T(2,128)S(1)} collective-permute-done((f32[7,2,5,256]{3,1,2,0:T(2,128)S(1)}, f32[7,2,5,256]{3,1,2,0:T(2,128)S(1)}, u32[]{:S(2)}, u32[]{:S(2)}) %collective-permute-start.4) | collective-permute-done | bytes 71712 | tf_op jit(solution)/shard_map/ppermute | solution.py:21
  101.7 14.2 %all_gather.20 = f32[28,2,5,256]{3,1,2,0:T(2,128)S(1)} all-gather(f32[7,2,5,256]{3,1,2,0:T(2,128)S(1)} %collective-permute-done.4), channel_id=1, replica_groups=mesh['row'=4,'col'=8] {'row'}, dimensions={0}, use_global_device_ids=true | all-gather | bytes 358400 | tf_op jit(solution)/shard_map/all_gather | solution.py:241
  117.1 14.4 %all_gather.21 = f32[28,2,5,256]{3,1,2,0:T(2,128)S(1)} all-gather(f32[7,2,5,256]{3,1,2,0:T(2,128)S(1)} %collective-permute-done.5), channel_id=1, replica_groups=mesh['row'=4,'col'=8] {'row'}, dimensions={0}, use_global_device_ids=true | all-gather | bytes 358400 | tf_op jit(solution)/shard_map/all_gather | solution.py:242
  139.6 3.6 %collective-permute-done.6 = f32[7,2,5,256]{3,1,2,0:T(2,128)S(1)} collective-permute-done((f32[7,2,5,256]{3,1,2,0:T(2,128)S(1)}, f32[7,2,5,256]{3,1,2,0:T(2,128)S(1)}, u32[]{:S(2)}, u32[]{:S(2)}) %collective-permute-start.6) | collective-permute-done | bytes 71712 | tf_op jit(solution)/shard_map/ppermute | solution.py:21
  143.2 14.1 %all_gather.22 = f32[28,2,5,256]{3,1,2,0:T(2,128)S(1)} all-gather(f32[7,2,5,256]{3,1,2,0:T(2,128)S(1)} %collective-permute-done.6), channel_id=1, replica_groups=mesh['row'=4,'col'=8] {'row'}, dimensions={0}, use_global_device_ids=true | all-gather | bytes 358400 | tf_op jit(solution)/shard_map/all_gather | solution.py:241
  158.6 14.4 %all_gather.23 = f32[28,2,5,256]{3,1,2,0:T(2,128)S(1)} all-gather(f32[7,2,5,256]{3,1,2,0:T(2,128)S(1)} %collective-permute-done.7), channel_id=1, replica_groups=mesh['row'=4,'col'=8] {'row'}, dimensions={0}, use_global_device_ids=true | all-gather | bytes 358400 | tf_op jit(solution)/shard_map/all_gather | solution.py:242
  178.9 0.8 copy.184
  (265 shorter events, 36.6 us)
Async XLA Ops:
  9.0 18.9 %collective-permute-start = (f32[5,5,16,256]{3,2,1,0:T(8,128)S(1)}, f32[5,5,16,256]{3,2,1,0:T(8,128)S(1)}, u32[]{:S(2)}, u32[]{:S(2)}) collective-permute-start(f32[5,5,16,256]{3,2,1,0:T(8,128)S(1)} %broadcast_select_fusion.2), channel_id=1, source_target_pairs={{0,8},{8,0},{16,24},{24,16},{1,9},{9,1},{17,25},{25,17},{2,10},{10... | collective-permute-start | bytes 1228808 | tf_op jit(solution)/shard_map/ppermute | solution.py:15
  22.2 5.7 %copy-start = (f32[11,5,16,256]{3,2,1,0:T(8,128)S(1)}, f32[11,5,16,256]{3,2,1,0:T(8,128)}, u32[]{:S(2)}) copy-start(f32[11,5,16,256]{3,2,1,0:T(8,128)} %param.45) | copy-start | bytes 2703364
  29.5 20.5 %collective-permute-start.1 = (f32[5,5,16,256]{3,2,1,0:T(8,128)S(1)}, f32[5,5,16,256]{3,2,1,0:T(8,128)S(1)}, u32[]{:S(2)}, u32[]{:S(2)}) collective-permute-start(f32[5,5,16,256]{3,2,1,0:T(8,128)S(1)} %broadcast_select_fusion.1), channel_id=1, source_target_pairs={{0,16},{8,24},{16,0},{24,8},{1,17},{9,25},{17,1},{25,9},{2,18},{10... | collective-permute-start | bytes 1228808 | tf_op jit(solution)/shard_map/ppermute | solution.py:15
  50.1 0.7 copy-start.2
  52.2 22.2 %collective-permute-start.3 = (f32[7,2,5,256]{3,1,2,0:T(2,128)S(1)}, f32[7,2,5,256]{3,1,2,0:T(2,128)S(1)}, u32[]{:S(2)}, u32[]{:S(2)}) collective-permute-start(f32[7,2,5,256]{3,1,2,0:T(2,128)S(1)} %pad_maximum_fusion.29), channel_id=1, source_target_pairs={{1,0},{2,1},{3,2},{4,3},{5,4},{6,5},{7,6},{0,7},{9,8},{10,9},{11,1... | collective-permute-start | bytes 215048 | tf_op jit(solution)/shard_map/ppermute | solution.py:21
  54.5 4.7 %collective-permute-start.2 = (f32[7,2,5,256]{3,1,2,0:T(2,128)S(1)}, f32[7,2,5,256]{3,1,2,0:T(2,128)S(1)}, u32[]{:S(2)}, u32[]{:S(2)}) collective-permute-start(f32[7,2,5,256]{3,1,2,0:T(2,128)S(1)} %pad_maximum_fusion.28), channel_id=1, source_target_pairs={{7,0},{0,1},{1,2},{2,3},{3,4},{4,5},{5,6},{6,7},{15,8},{8,9},{9,10... | collective-permute-start | bytes 215048 | tf_op jit(solution)/shard_map/ppermute | solution.py:21
  88.4 0.8 copy-start.1
  96.6 20.5 %collective-permute-start.5 = (f32[7,2,5,256]{3,1,2,0:T(2,128)S(1)}, f32[7,2,5,256]{3,1,2,0:T(2,128)S(1)}, u32[]{:S(2)}, u32[]{:S(2)}) collective-permute-start(f32[7,2,5,256]{3,1,2,0:T(2,128)S(1)} %pad_maximum_fusion.31), channel_id=1, source_target_pairs={{1,0},{2,1},{3,2},{4,3},{5,4},{6,5},{7,6},{0,7},{9,8},{10,9},{11,1... | collective-permute-start | bytes 215048 | tf_op jit(solution)/shard_map/ppermute | solution.py:21
  96.8 4.9 %collective-permute-start.4 = (f32[7,2,5,256]{3,1,2,0:T(2,128)S(1)}, f32[7,2,5,256]{3,1,2,0:T(2,128)S(1)}, u32[]{:S(2)}, u32[]{:S(2)}) collective-permute-start(f32[7,2,5,256]{3,1,2,0:T(2,128)S(1)} %pad_maximum_fusion.30), channel_id=1, source_target_pairs={{7,0},{0,1},{1,2},{2,3},{3,4},{4,5},{5,6},{6,7},{15,8},{8,9},{9,10... | collective-permute-start | bytes 215048 | tf_op jit(solution)/shard_map/ppermute | solution.py:21
  138.3 20.2 %collective-permute-start.7 = (f32[7,2,5,256]{3,1,2,0:T(2,128)S(1)}, f32[7,2,5,256]{3,1,2,0:T(2,128)S(1)}, u32[]{:S(2)}, u32[]{:S(2)}) collective-permute-start(f32[7,2,5,256]{3,1,2,0:T(2,128)S(1)} %pad_maximum_fusion.33), channel_id=1, source_target_pairs={{1,0},{2,1},{3,2},{4,3},{5,4},{6,5},{7,6},{0,7},{9,8},{10,9},{11,1... | collective-permute-start | bytes 215048 | tf_op jit(solution)/shard_map/ppermute | solution.py:21
  138.5 4.7 %collective-permute-start.6 = (f32[7,2,5,256]{3,1,2,0:T(2,128)S(1)}, f32[7,2,5,256]{3,1,2,0:T(2,128)S(1)}, u32[]{:S(2)}, u32[]{:S(2)}) collective-permute-start(f32[7,2,5,256]{3,1,2,0:T(2,128)S(1)} %pad_maximum_fusion.32), channel_id=1, source_target_pairs={{7,0},{0,1},{1,2},{2,3},{3,4},{4,5},{5,6},{6,7},{15,8},{8,9},{9,10... | collective-permute-start | bytes 215048 | tf_op jit(solution)/shard_map/ppermute | solution.py:21
where the time goes:
time: 180 us
  blocking collectives  85.5 us (48%)
  local copies, waits for them, and re-layouts  32.5 us (18%)
  waiting for transfers between devices  29.1 us (16%)
  other arithmetic  19.2 us (11%)
  starting transfers between devices  9.39 us (5%)
  between operations  3.94 us (2%)
    all_gather x3, blocking collectives, section_rate(): lax.all_gather(passed_highs, 'row', axis=0, tiled=True)  42.9 us
    all_gather x3, blocking collectives, section_rate(): lax.all_gather(passed_lows, 'row', axis=0, tiled=True)  42.7 us
    ppermute x2, waiting for transfers between devices, swapped(): lax.ppermute(array, axis, [(i, i ^ 1 << apart) for i in range(lax.axis_si...  17.8 us
    ppermute x6, waiting for transfers between devices, from_behind(): return lax.ppermute(block, axis, route)  11.3 us
    gather x6, local copies, waits for them, and re-layouts, rebalance_table(): jnp.take_along_axis(other_anchors, jnp.clip(anchor_slot, 0, slot_width -...  8.44 us
    ppermute x2, starting transfers between devices, swapped(): lax.ppermute(array, axis, [(i, i ^ 1 << apart) for i in range(lax.axis_si...  5.78 us
    sub x9, other arithmetic, face_flux(): 0.5 * (lower_data[0] + upper_data[0])  3.63 us
    ppermute x6, starting transfers between devices, from_behind(): return lax.ppermute(block, axis, route)  3.61 us
  transfers between devices with their start and end apart: 8, of which 4 were waited for; matrix products, arithmetic and copies ran while one was open for 11% of the time, Pallas kernels for 0%

commit v1 on v0

--- a/solution.py
+++ b/solution.py
@@ -238,7 +238,9 @@
         passed_highs = from_behind(highs, "col", 1)
         passed_lows = from_behind(lows, "col", -1)
         from_below, from_above = (
-            lax.all_gather(passed_highs, "row", axis=0, tiled=True),
+            jnp.concatenate(
+                lax.all_to_all(jnp.stack(lax.axis_size("row") * [passed_highs]), "row", 0, 0), 0
+            ),
             lax.all_gather(passed_lows, "row", axis=0, tiled=True),
         )
         low_x = from_below[from_x_low, 0][:, :, None, :]

time: 180 us -> 159 us (0.88)
  blocking collectives: 85.5 us -> 47.3 us
  starting transfers between devices: 9.39 us -> 19.7 us
  local copies, waits for them, and re-layouts: 32.5 us -> 36.7 us
  waiting for transfers between devices: 29.1 us -> 31 us
    all_gather x3 -> x0, blocking collectives: 42.9 us -> none  [section_rate(): lax.all_gather(passed_highs, 'row', axis=0, tiled=True)]
    all_to_all x0 -> x3, starting transfers between devices: none -> 10.5 us  [section_rate(): lax.all_to_all(jnp.stack(lax.axis_size('row') * [passed_highs]), 'row', 0...]
    all_gather x3, blocking collectives: 42.7 us -> 47.3 us  [section_rate(): lax.all_gather(passed_lows, 'row', axis=0, tiled=True)]
    another operation x2 -> x5, local copies, waits for them, and re-layouts: 0.01 us -> 2.37 us  [the longest x3 2.36 us: section_rate(): jnp.stack(lax.axis_size('row') * [passed_highs])]
    ppermute x6, waiting for transfers between devices: 11.3 us -> 13.2 us  [from_behind(): return lax.ppermute(block, axis, route)]
  transfers between devices with their start and end apart: 8 -> 11, of which waited for: 4 -> 4; matrix products, arithmetic and copies ran while one was open for 11% -> 16% of each run, Pallas kernels for 0% -> 0%
where the time goes in v1:
time: 159 us; the launch traced here: 158 us
  blocking collectives  47.3 us (30%)
  local copies, waits for them, and re-layouts  36.7 us (23%)
  waiting for transfers between devices  31 us (19%)
  starting transfers between devices  19.7 us (12%)
  other arithmetic  19.3 us (12%)
  between operations  4.41 us (3%)
    all_gather x3, blocking collectives, section_rate(): lax.all_gather(passed_lows, 'row', axis=0, tiled=True)  47.3 us
    ppermute x2, waiting for transfers between devices, swapped(): lax.ppermute(array, axis, [(i, i ^ 1 << apart) for i in range(lax.axis_si...  17.8 us
    ppermute x6, waiting for transfers between devices, from_behind(): return lax.ppermute(block, axis, route)  13.2 us
    all_to_all x3, starting transfers between devices, section_rate(): lax.all_to_all(jnp.stack(lax.axis_size('row') * [passed_highs]), 'row', 0...  10.5 us
    gather x6, local copies, waits for them, and re-layouts, rebalance_table(): jnp.take_along_axis(other_anchors, jnp.clip(anchor_slot, 0, slot_width -...  8.44 us
    ppermute x2, starting transfers between devices, swapped(): lax.ppermute(array, axis, [(i, i ^ 1 << apart) for i in range(lax.axis_si...  5.78 us
    sub x9, other arithmetic, face_flux(): 0.5 * (lower_data[0] + upper_data[0])  3.66 us
    ppermute x6, starting transfers between devices, from_behind(): return lax.ppermute(block, axis, route)  3.43 us
  transfers between devices with their start and end apart: 11, of which 4 were waited for; matrix products, arithmetic and copies ran while one was open for 16% of the time, Pallas kernels for 0%

profile of v1, /device:TPU:0, one launch (start us, length us, event | category | flops | bytes accessed | tf_op | source)
XLA Modules:
  0.0 158.4 jit_solution(4212053589018604607)
XLA Ops:
  0.0 0.8 copy.142
  7.5 1.7 %gather_fusion.21 = f32[5,5,16,256]{3,2,1,0:T(8,128)S(1)} fusion(f32[11,5,16,256]{3,2,1,0:T(8,128)} %param.45, s32[1024]{0:T(1024)S(1)} %pad_clamp_fusion.6), kind=kCustom, calls=%fused_computation.1.clone | custom fusion | bytes 819220 | tf_op jit(solution)/shard_map/jit(_take)/gather | solution.py:197
  9.4 3.1 %collective-permute-start = (f32[5,5,16,256]{3,2,1,0:T(8,128)S(1)}, f32[5,5,16,256]{3,2,1,0:T(8,128)S(1)}, u32[]{:S(2)}, u32[]{:S(2)}) collective-permute-start(f32[5,5,16,256]{3,2,1,0:T(8,128)S(1)} %broadcast_select_fusion.2), channel_id=1, source_target_pairs={{0,8},{8,0},{16,24},{24,16},{1,9},{9,1},{17,25},{25,17},{2,10},{10... | collective-permute-start | bytes 1228808 | tf_op jit(solution)/shard_map/ppermute | solution.py:15
  13.7 4.0 %gather_fusion.19 = s32[352]{0:T(512)S(1)} fusion(s32[4,8,11]{2,1,0:T(8,128)S(1)} %gather_fusion.2, s32[352]{0:T(512)S(1)} %reshape.1182), kind=kCustom, calls=%fused_computation.clone | custom fusion | bytes 7040 | tf_op jit(solution)/shard_map/jit(take_along_axis)/gather | solution.py:36
  18.5 4.0 %gather_fusion.20 = s32[352]{0:T(512)S(1)} fusion(s32[4,8,11]{2,1,0:T(8,128)S(1)} %gather_fusion.3, s32[352]{0:T(512)S(1)} %reshape.1187), kind=kCustom, calls=%fused_computation.3.clone | custom fusion | bytes 7040 | tf_op jit(solution)/shard_map/jit(take_along_axis)/gather | solution.py:36
  23.3 0.7 gather_fusion.7
  24.0 0.7 gather_fusion.4
  30.4 2.7 %collective-permute-start.1 = (f32[5,5,16,256]{3,2,1,0:T(8,128)S(1)}, f32[5,5,16,256]{3,2,1,0:T(8,128)S(1)}, u32[]{:S(2)}, u32[]{:S(2)}) collective-permute-start(f32[5,5,16,256]{3,2,1,0:T(8,128)S(1)} %broadcast_select_fusion.1), channel_id=1, source_target_pairs={{0,16},{8,24},{16,0},{24,8},{1,17},{9,25},{17,1},{25,9},{2,18},{10... | collective-permute-start | bytes 1228808 | tf_op jit(solution)/shard_map/ppermute | solution.py:15
  33.1 17.8 %collective-permute-done.1 = f32[5,5,16,256]{3,2,1,0:T(8,128)S(1)} collective-permute-done((f32[5,5,16,256]{3,2,1,0:T(8,128)S(1)}, f32[5,5,16,256]{3,2,1,0:T(8,128)S(1)}, u32[]{:S(2)}, u32[]{:S(2)}) %collective-permute-start.1) | collective-permute-done | bytes 409632 | tf_op jit(solution)/shard_map/ppermute | solution.py:15
  53.1 2.2 %collective-permute-start.3 = (f32[7,2,5,256]{3,1,2,0:T(2,128)S(1)}, f32[7,2,5,256]{3,1,2,0:T(2,128)S(1)}, u32[]{:S(2)}, u32[]{:S(2)}) collective-permute-start(f32[7,2,5,256]{3,1,2,0:T(2,128)S(1)} %pad_maximum_fusion.29), channel_id=1, source_target_pairs={{1,0},{2,1},{3,2},{4,3},{5,4},{6,5},{7,6},{0,7},{9,8},{10,9},{11,1... | collective-permute-start | bytes 215048 | tf_op jit(solution)/shard_map/ppermute | solution.py:21
  55.5 4.6 %collective-permute-done.2 = f32[7,2,5,256]{3,1,2,0:T(2,128)S(1)} collective-permute-done((f32[7,2,5,256]{3,1,2,0:T(2,128)S(1)}, f32[7,2,5,256]{3,1,2,0:T(2,128)S(1)}, u32[]{:S(2)}, u32[]{:S(2)}) %collective-permute-start.2) | collective-permute-done | bytes 71712 | tf_op jit(solution)/shard_map/ppermute | solution.py:21
  60.1 0.8 stack.25
  60.9 3.5 %all-to-all-start = ((f32[4,7,2,5,256]{4,2,3,1,0:T(2,128)}), f32[4,7,2,5,256]{4,2,3,1,0:T(2,128)S(1)}, u32[]{:S(2)}, u32[]{:S(2)}) async-start(f32[4,7,2,5,256]{4,2,3,1,0:T(2,128)} %stack.25), calls=%async_computation | async-start | bytes 573440 | tf_op jit(solution)/shard_map/all_to_all | solution.py:242
  64.9 15.9 %all_gather.9 = f32[28,2,5,256]{3,1,2,0:T(2,128)S(1)} all-gather(f32[7,2,5,256]{3,1,2,0:T(2,128)S(1)} %collective-permute-done.3), channel_id=1, replica_groups=mesh['row'=4,'col'=8] {'row'}, dimensions={0}, use_global_device_ids=true | all-gather | bytes 358400 | tf_op jit(solution)/shard_map/all_gather | solution.py:244
  83.6 1.6 %gather_fusion.6 = f32[7,5,256]{2,1,0:T(8,128)S(1)} fusion(f32[28,2,5,256]{3,2,1,0:T(8,128)} %bitcast.410, s32[7]{0:T(128)S(1)} %get-tuple-element.342), kind=kCustom, calls=%fused_computation.12 | custom fusion | bytes 71736 | tf_op jit(solution)/shard_map/gather | solution.py:246
  90.9 4.3 %collective-permute-done.4 = f32[7,2,5,256]{3,1,2,0:T(2,128)S(1)} collective-permute-done((f32[7,2,5,256]{3,1,2,0:T(2,128)S(1)}, f32[7,2,5,256]{3,1,2,0:T(2,128)S(1)}, u32[]{:S(2)}, u32[]{:S(2)}) %collective-permute-start.4) | collective-permute-done | bytes 71712 | tf_op jit(solution)/shard_map/ppermute | solution.py:21
  95.3 0.8 stack.56
  96.1 3.6 %all-to-all-start.1 = ((f32[4,7,2,5,256]{4,2,3,1,0:T(2,128)}), f32[4,7,2,5,256]{4,2,3,1,0:T(2,128)S(1)}, u32[]{:S(2)}, u32[]{:S(2)}) async-start(f32[4,7,2,5,256]{4,2,3,1,0:T(2,128)} %stack.56), calls=%async_computation.1 | async-start | bytes 573440 | tf_op jit(solution)/shard_map/all_to_all | solution.py:242
  100.2 15.6 %all_gather.10 = f32[28,2,5,256]{3,1,2,0:T(2,128)S(1)} all-gather(f32[7,2,5,256]{3,1,2,0:T(2,128)S(1)} %collective-permute-done.5), channel_id=1, replica_groups=mesh['row'=4,'col'=8] {'row'}, dimensions={0}, use_global_device_ids=true | all-gather | bytes 358400 | tf_op jit(solution)/shard_map/all_gather | solution.py:244
  124.7 4.2 %collective-permute-done.6 = f32[7,2,5,256]{3,1,2,0:T(2,128)S(1)} collective-permute-done((f32[7,2,5,256]{3,1,2,0:T(2,128)S(1)}, f32[7,2,5,256]{3,1,2,0:T(2,128)S(1)}, u32[]{:S(2)}, u32[]{:S(2)}) %collective-permute-start.6) | collective-permute-done | bytes 71712 | tf_op jit(solution)/shard_map/ppermute | solution.py:21
  128.9 0.8 stack.60
  129.7 3.5 %all-to-all-start.2 = ((f32[4,7,2,5,256]{4,2,3,1,0:T(2,128)}), f32[4,7,2,5,256]{4,2,3,1,0:T(2,128)S(1)}, u32[]{:S(2)}, u32[]{:S(2)}) async-start(f32[4,7,2,5,256]{4,2,3,1,0:T(2,128)} %stack.60), calls=%async_computation.2 | async-start | bytes 573440 | tf_op jit(solution)/shard_map/all_to_all | solution.py:242
  133.8 15.8 %all_gather.11 = f32[28,2,5,256]{3,1,2,0:T(2,128)S(1)} all-gather(f32[7,2,5,256]{3,1,2,0:T(2,128)S(1)} %collective-permute-done.7), channel_id=1, replica_groups=mesh['row'=4,'col'=8] {'row'}, dimensions={0}, use_global_device_ids=true | all-gather | bytes 358400 | tf_op jit(solution)/shard_map/all_gather | solution.py:244
  157.6 0.8 copy.181
  (303 shorter events, 40.4 us)
Async XLA Ops:
  9.4 19.5 %collective-permute-start = (f32[5,5,16,256]{3,2,1,0:T(8,128)S(1)}, f32[5,5,16,256]{3,2,1,0:T(8,128)S(1)}, u32[]{:S(2)}, u32[]{:S(2)}) collective-permute-start(f32[5,5,16,256]{3,2,1,0:T(8,128)S(1)} %broadcast_select_fusion.2), channel_id=1, source_target_pairs={{0,8},{8,0},{16,24},{24,16},{1,9},{9,1},{17,25},{25,17},{2,10},{10... | collective-permute-start | bytes 1228808 | tf_op jit(solution)/shard_map/ppermute | solution.py:15
  12.5 109.7 %copy-start.12 = (pred[256]{0:T(512)(128)(4,1)}, pred[256]{0:T(512)(128)(4,1)S(1)}, u32[]{:S(2)}) copy-start(pred[256]{0:T(512)(128)(4,1)S(1)} %get-tuple-element.346) | copy-start | bytes 772
  12.5 109.7 %copy-start.14 = (pred[256]{0:T(512)(128)(4,1)}, pred[256]{0:T(512)(128)(4,1)S(1)}, u32[]{:S(2)}) copy-start(pred[256]{0:T(512)(128)(4,1)S(1)} %get-tuple-element.347) | copy-start | bytes 772
  22.5 6.3 %copy-start = (f32[11,5,16,256]{3,2,1,0:T(8,128)S(1)}, f32[11,5,16,256]{3,2,1,0:T(8,128)}, u32[]{:S(2)}) copy-start(f32[11,5,16,256]{3,2,1,0:T(8,128)} %param.45) | copy-start | bytes 2703364
  22.7 28.9 %copy-start.10 = (pred[7]{0:T(512)(128)(4,1)}, pred[7]{0:T(512)(128)(4,1)S(1)}, u32[]{:S(2)}) copy-start(pred[7]{0:T(512)(128)(4,1)S(1)} %compare_bitcast_fusion) | copy-start | bytes 25
  30.4 20.5 %collective-permute-start.1 = (f32[5,5,16,256]{3,2,1,0:T(8,128)S(1)}, f32[5,5,16,256]{3,2,1,0:T(8,128)S(1)}, u32[]{:S(2)}, u32[]{:S(2)}) collective-permute-start(f32[5,5,16,256]{3,2,1,0:T(8,128)S(1)} %broadcast_select_fusion.1), channel_id=1, source_target_pairs={{0,16},{8,24},{16,0},{24,8},{1,17},{9,25},{17,1},{25,9},{2,18},{10... | collective-permute-start | bytes 1228808 | tf_op jit(solution)/shard_map/ppermute | solution.py:15
  33.0 82.8 %copy-start.8 = (s32[7]{0:T(128)}, s32[7]{0:T(128)S(1)}, u32[]{:S(2)}) copy-start(s32[7]{0:T(128)S(1)} %get-tuple-element.345) | copy-start | bytes 88
  33.0 83.4 %copy-start.6 = (s32[7]{0:T(128)}, s32[7]{0:T(128)S(1)}, u32[]{:S(2)}) copy-start(s32[7]{0:T(128)S(1)} %get-tuple-element.344) | copy-start | bytes 88
  33.1 84.3 %copy-start.4 = (s32[7]{0:T(128)}, s32[7]{0:T(128)S(1)}, u32[]{:S(2)}) copy-start(s32[7]{0:T(128)S(1)} %get-tuple-element.343) | copy-start | bytes 88
  33.1 84.9 %copy-start.2 = (s32[7]{0:T(128)}, s32[7]{0:T(128)S(1)}, u32[]{:S(2)}) copy-start(s32[7]{0:T(128)S(1)} %get-tuple-element.342) | copy-start | bytes 88
  53.1 11.7 %collective-permute-start.3 = (f32[7,2,5,256]{3,1,2,0:T(2,128)S(1)}, f32[7,2,5,256]{3,1,2,0:T(2,128)S(1)}, u32[]{:S(2)}, u32[]{:S(2)}) collective-permute-start(f32[7,2,5,256]{3,1,2,0:T(2,128)S(1)} %pad_maximum_fusion.29), channel_id=1, source_target_pairs={{1,0},{2,1},{3,2},{4,3},{5,4},{6,5},{7,6},{0,7},{9,8},{10,9},{11,1... | collective-permute-start | bytes 215048 | tf_op jit(solution)/shard_map/ppermute | solution.py:21
  55.4 4.7 %collective-permute-start.2 = (f32[7,2,5,256]{3,1,2,0:T(2,128)S(1)}, f32[7,2,5,256]{3,1,2,0:T(2,128)S(1)}, u32[]{:S(2)}, u32[]{:S(2)}) collective-permute-start(f32[7,2,5,256]{3,1,2,0:T(2,128)S(1)} %pad_maximum_fusion.28), channel_id=1, source_target_pairs={{7,0},{0,1},{1,2},{2,3},{3,4},{4,5},{5,6},{6,7},{15,8},{8,9},{9,10... | collective-permute-start | bytes 215048 | tf_op jit(solution)/shard_map/ppermute | solution.py:21
  60.9 21.4 %all-to-all-start = ((f32[4,7,2,5,256]{4,2,3,1,0:T(2,128)}), f32[4,7,2,5,256]{4,2,3,1,0:T(2,128)S(1)}, u32[]{:S(2)}, u32[]{:S(2)}) async-start(f32[4,7,2,5,256]{4,2,3,1,0:T(2,128)} %stack.25), calls=%async_computation | async-start | bytes 573440 | tf_op jit(solution)/shard_map/all_to_all | solution.py:242
  82.3 0.8 copy-start.1
  90.2 10.0 %collective-permute-start.5 = (f32[7,2,5,256]{3,1,2,0:T(2,128)S(1)}, f32[7,2,5,256]{3,1,2,0:T(2,128)S(1)}, u32[]{:S(2)}, u32[]{:S(2)}) collective-permute-start(f32[7,2,5,256]{3,1,2,0:T(2,128)S(1)} %pad_maximum_fusion.31), channel_id=1, source_target_pairs={{1,0},{2,1},{3,2},{4,3},{5,4},{6,5},{7,6},{0,7},{9,8},{10,9},{11,1... | collective-permute-start | bytes 215048 | tf_op jit(solution)/shard_map/ppermute | solution.py:21
  90.3 4.9 %collective-permute-start.4 = (f32[7,2,5,256]{3,1,2,0:T(2,128)S(1)}, f32[7,2,5,256]{3,1,2,0:T(2,128)S(1)}, u32[]{:S(2)}, u32[]{:S(2)}) collective-permute-start(f32[7,2,5,256]{3,1,2,0:T(2,128)S(1)} %pad_maximum_fusion.30), channel_id=1, source_target_pairs={{7,0},{0,1},{1,2},{2,3},{3,4},{4,5},{5,6},{6,7},{15,8},{8,9},{9,10... | collective-permute-start | bytes 215048 | tf_op jit(solution)/shard_map/ppermute | solution.py:21
  96.1 21.2 %all-to-all-start.1 = ((f32[4,7,2,5,256]{4,2,3,1,0:T(2,128)}), f32[4,7,2,5,256]{4,2,3,1,0:T(2,128)S(1)}, u32[]{:S(2)}, u32[]{:S(2)}) async-start(f32[4,7,2,5,256]{4,2,3,1,0:T(2,128)} %stack.56), calls=%async_computation.1 | async-start | bytes 573440 | tf_op jit(solution)/shard_map/all_to_all | solution.py:242
  124.0 9.8 %collective-permute-start.7 = (f32[7,2,5,256]{3,1,2,0:T(2,128)S(1)}, f32[7,2,5,256]{3,1,2,0:T(2,128)S(1)}, u32[]{:S(2)}, u32[]{:S(2)}) collective-permute-start(f32[7,2,5,256]{3,1,2,0:T(2,128)S(1)} %pad_maximum_fusion.33), channel_id=1, source_target_pairs={{1,0},{2,1},{3,2},{4,3},{5,4},{6,5},{7,6},{0,7},{9,8},{10,9},{11,1... | collective-permute-start | bytes 215048 | tf_op jit(solution)/shard_map/ppermute | solution.py:21
  124.1 4.8 %collective-permute-start.6 = (f32[7,2,5,256]{3,1,2,0:T(2,128)S(1)}, f32[7,2,5,256]{3,1,2,0:T(2,128)S(1)}, u32[]{:S(2)}, u32[]{:S(2)}) collective-permute-start(f32[7,2,5,256]{3,1,2,0:T(2,128)S(1)} %pad_maximum_fusion.32), channel_id=1, source_target_pairs={{7,0},{0,1},{1,2},{2,3},{3,4},{4,5},{5,6},{6,7},{15,8},{8,9},{9,10... | collective-permute-start | bytes 215048 | tf_op jit(solution)/shard_map/ppermute | solution.py:21
  129.7 21.3 %all-to-all-start.2 = ((f32[4,7,2,5,256]{4,2,3,1,0:T(2,128)}), f32[4,7,2,5,256]{4,2,3,1,0:T(2,128)S(1)}, u32[]{:S(2)}, u32[]{:S(2)}) async-start(f32[4,7,2,5,256]{4,2,3,1,0:T(2,128)} %stack.60), calls=%async_computation.2 | async-start | bytes 573440 | tf_op jit(solution)/shard_map/all_to_all | solution.py:242
  133.6 16.1 %copy-start.9 = (s32[7]{0:T(128)S(1)}, s32[7]{0:T(128)}, u32[]{:S(2)}) copy-start(s32[7]{0:T(128)} %copy-done.8) | copy-start | bytes 88
  133.6 16.7 %copy-start.7 = (s32[7]{0:T(128)S(1)}, s32[7]{0:T(128)}, u32[]{:S(2)}) copy-start(s32[7]{0:T(128)} %copy-done.6) | copy-start | bytes 88
  133.7 17.4 %copy-start.5 = (s32[7]{0:T(128)S(1)}, s32[7]{0:T(128)}, u32[]{:S(2)}) copy-start(s32[7]{0:T(128)} %copy-done.4) | copy-start | bytes 88
  133.7 18.0 %copy-start.3 = (s32[7]{0:T(128)S(1)}, s32[7]{0:T(128)}, u32[]{:S(2)}) copy-start(s32[7]{0:T(128)} %copy-done.2) | copy-start | bytes 88
  (6 other events, 4.0 us)
